TPU v7x, 512 devices: a whole 4x4x16 slice. The times are simulated.
512 devices in a mesh: rep: 64 (over x_lo, z, core), tp: 8 (over y, x_hi).
Axes of the slice: x: 4 (x_hi: 2, x_lo: 2; x = x_hi * 2 + x_lo), y: 4, z: 16, core: 2. Of those that a mesh axis runs over, the one named last changes fastest.
Arguments:
- prompt_q: bfloat16 [32768, 2048], P('rep', 'tp'), may hold values from -24 to 24
- prompt_k: bfloat16 [32768, 2048], P('rep', 'tp'), may hold values from -24 to 24
- prompt_v: bfloat16 [32768, 2048], P('rep', 'tp'), may hold values from -6 to 6
- prompt_len: int32 [64], P('rep'), may hold values from 256 to 512, as said below
- cache_keys: bfloat16 [128, 1024, 2048], P('rep', None, 'tp'), may hold values from -24 to 24
- cache_values: bfloat16 [128, 1024, 2048], P('rep', None, 'tp'), may hold values from -6 to 6
- new_q: bfloat16 [128, 2048], P('rep', 'tp'), may hold values from -24 to 24
- new_k: bfloat16 [128, 2048], P('rep', 'tp'), may hold values from -6 to 6
- new_v: bfloat16 [128, 2048], P('rep', 'tp'), may hold values from -6 to 6
- cache_len: int32 [128], replicated, may hold values from 260 to 1024, as said below
- moving: int32 [64], replicated, may hold values from 0 to 1
- out_weight: bfloat16 [2048, 2048], P(None, 'tp'), may hold values from -0.125 to 0.125
- out_bias: float32 [2048], P('tp'), may hold values from -1.75 to 1.75
- residual: bfloat16 [32896, 2048], P('rep', 'tp'), may hold values from -150 to 150
- ln_gain: float32 [2048], P('tp'), may hold values from 0.1 to 1.9
- ln_shift: float32 [2048], P('tp'), may hold values from -1.75 to 1.75
Outputs:
- hidden_out: bfloat16 [32896, 2048], P('rep', 'tp')
- normed: bfloat16 [32896, 2048], P('rep', 'tp')
- moved_window: bfloat16 [64, 2, 260, 2048], P('rep', None, None, 'tp')
Inputs may be any that keep to these rules, and one draw needn't show every extreme that they name: `prompt_len`: some replica's prompt has all 512 tokens live. `cache_len`: some request's cache is full.
All inputs are finite; a program needn't handle non-finite values.
Results may differ from a plain program's by a relative error of at most 0.0022.
Values may be sent and summed in bfloat16 or wider, within the bound.
No kernel may reach another device: no remote copies, remote signals or barrier semaphores. Data moves between devices by JAX's collectives and lax.ppermute only.
A program may use at most 64 MiB of HBM per device.

v0:
```python
import math
import jax
import jax.numpy as jnp
from jax import lax
from jax.sharding import PartitionSpec as P

D = 2048
HEADS = 16
HD = 128
SINK = 4
WIN = 256
masked_score = -1e30
norm_epsilon = 1e-05


def from_behind(block, axis, distance):
    devices = range(lax.axis_size(axis))
    route = [((i - distance) % len(devices), i) for i in devices]
    return lax.ppermute(block, axis, route)


def head_slopes(local_heads):
    first_head = lax.axis_index("tp") * local_heads
    head_ids = (first_head + jnp.arange(local_heads, dtype=jnp.int32)).astype(jnp.float32)
    return jnp.exp2(-8.0 * (head_ids + 1.0) / HEADS)


def softmax_rows(scores):
    row_max = jnp.max(scores, axis=-1, keepdims=True)
    expo_terms = jnp.exp(scores - row_max)
    return (expo_terms / jnp.sum(expo_terms, axis=-1, keepdims=True)).astype(jnp.bfloat16)


def prompt_attend(query_rows, key_rows, value_rows, length, slopes):
    row_count = query_rows.shape[0]
    local_heads = slopes.shape[0]
    query_heads = query_rows.reshape(row_count, local_heads, HD)
    key_heads = key_rows.reshape(row_count, local_heads, HD)
    value_heads = value_rows.reshape(row_count, local_heads, HD)
    scores = jnp.einsum(
        "qhd,khd->hqk", query_heads, key_heads, preferred_element_type=jnp.float32
    ) * (1.0 / math.sqrt(HD))
    position = jnp.arange(row_count, dtype=jnp.int32)
    distance = (position[:, None] - position[None, :]).astype(jnp.float32)
    scores = scores - slopes[:, None, None] * distance[None]
    allowed = (position[None, :] <= position[:, None]) & (position[None, :] < length)
    scores = jnp.where(allowed[None], scores, masked_score)
    weights = softmax_rows(scores)
    mixed_heads = jnp.einsum(
        "hqk,khd->qhd", weights, value_heads, preferred_element_type=jnp.float32
    )
    return mixed_heads.astype(jnp.bfloat16).reshape(row_count, local_heads * HD)


def window_rows(cache_rows, newest, length):
    middle = lax.dynamic_slice_in_dim(cache_rows, length + 1 - WIN, WIN - 1, 0)
    return jnp.concatenate([cache_rows[:SINK], middle, newest[None]], axis=0)


def window_positions(length):
    sink_part = jnp.arange(SINK, dtype=jnp.int32)
    tail_part = length + 1 - WIN + jnp.arange(WIN, dtype=jnp.int32)
    return jnp.concatenate([sink_part, tail_part])


def decode_attend(query_row, key_window, value_window, length, slopes):
    local_heads = slopes.shape[0]
    query_heads = query_row.reshape(local_heads, HD)
    key_heads = key_window.reshape(-1, local_heads, HD)
    value_heads = value_window.reshape(-1, local_heads, HD)
    scores = jnp.einsum(
        "hd,whd->hw", query_heads, key_heads, preferred_element_type=jnp.float32
    ) * (1.0 / math.sqrt(HD))
    distance = (length - window_positions(length)).astype(jnp.float32)
    scores = scores - slopes[:, None] * distance[None, :]
    weights = softmax_rows(scores)
    mixed_heads = jnp.einsum("hw,whd->hd", weights, value_heads, preferred_element_type=jnp.float32)
    return mixed_heads.astype(jnp.bfloat16).reshape(local_heads * HD)


def select_slot(stacked, slot_index):
    return lax.dynamic_index_in_dim(stacked, slot_index, 0, keepdims=False)


def on_device(
    prompt_q,
    prompt_k,
    prompt_v,
    prompt_len,
    cache_keys,
    cache_values,
    new_q,
    new_k,
    new_v,
    cache_len,
    moving,
    out_weight,
    out_bias,
    residual,
    ln_gain,
    ln_shift,
):
    replica_count = lax.axis_size("rep")
    replica_index = lax.axis_index("rep")
    partner = (replica_index + replica_count // 2) % replica_count
    local_heads = prompt_q.shape[1] // HD
    slopes = head_slopes(local_heads)
    prompt_mix = prompt_attend(prompt_q, prompt_k, prompt_v, prompt_len[0], slopes)
    slot_count = cache_keys.shape[0]
    leaving = moving[replica_index]
    staying = 1 - leaving
    stay_len = cache_len[replica_index * slot_count + staying]
    come_len = cache_len[partner * slot_count + moving[partner]]
    stay_keys = window_rows(select_slot(cache_keys, staying), select_slot(new_k, staying), stay_len)
    stay_values = window_rows(
        select_slot(cache_values, staying), select_slot(new_v, staying), stay_len
    )
    stay_out = decode_attend(select_slot(new_q, staying), stay_keys, stay_values, stay_len, slopes)
    come_cache_keys, come_cache_values, come_query, come_key, come_value = from_behind(
        (
            select_slot(cache_keys, leaving),
            select_slot(cache_values, leaving),
            select_slot(new_q, leaving),
            select_slot(new_k, leaving),
            select_slot(new_v, leaving),
        ),
        "rep",
        replica_count // 2,
    )
    come_keys = window_rows(come_cache_keys, come_key, come_len)
    come_values = window_rows(come_cache_values, come_value, come_len)
    come_out = decode_attend(come_query, come_keys, come_values, come_len, slopes)
    mixed_rows = jnp.concatenate([prompt_mix, stay_out[None], come_out[None]], axis=0)
    projected = jnp.dot(
        lax.all_gather(mixed_rows, "tp", axis=1, tiled=True),
        out_weight,
        preferred_element_type=jnp.float32,
    )
    stream = projected + out_bias[None, :] + residual.astype(jnp.float32)
    hidden_out = stream.astype(jnp.bfloat16)
    row_total = jnp.sum(stream, axis=1)
    row_mean = lax.psum(row_total, "tp") / D
    centered = stream - row_mean[:, None]
    row_var = lax.psum(jnp.sum(centered * centered, axis=1), "tp") / D
    normed = (
        centered * lax.rsqrt(row_var + norm_epsilon)[:, None] * ln_gain[None, :] + ln_shift[None, :]
    ).astype(jnp.bfloat16)
    moved_window = jnp.stack([come_keys, come_values], axis=0)[None]
    return (hidden_out, normed, moved_window)


def solution(mesh):
    in_specs = (
        P("rep", "tp"),
        P("rep", "tp"),
        P("rep", "tp"),
        P("rep"),
        P("rep", None, "tp"),
        P("rep", None, "tp"),
        P("rep", "tp"),
        P("rep", "tp"),
        P("rep", "tp"),
        P(),
        P(),
        P(None, "tp"),
        P("tp"),
        P("rep", "tp"),
        P("tp"),
        P("tp"),
    )
    out_specs = (P("rep", "tp"), P("rep", "tp"), P("rep", None, None, "tp"))
    return jax.shard_map(
        on_device, mesh=mesh, in_specs=in_specs, out_specs=out_specs, check_vma=False
    )
```

profile of v0, /device:TPU:32, one launch (start us, length us, event | category | flops | bytes accessed | tf_op | source)
XLA Modules:
  0.0 192.9 jit_solution(14140378695549050792)
XLA Ops:
  7.3 1.3 fusion.47
  10.6 1.1 dynamic-slice_bitcast_fusion.1
  11.6 3.4 %collective-permute-start.1 = (bf16[1024,256]{1,0:T(8,128)(2,1)S(1)}, bf16[1024,256]{1,0:T(8,128)(2,1)}, u32[]{:S(2)}, u32[]{:S(2)}) collective-permute-start(bf16[1024,256]{1,0:T(8,128)(2,1)S(1)} %dynamic-slice_bitcast_fusion.1), channel_id=1, source_target_pairs={{256,0},{264,8},{272,16},{280,24},{288,32},{296,40},{304,48},{312,... | collective-permute-start | bytes 1572872 | tf_op jit(solution)/shard_map/ppermute | solution.py:19
  16.3 1.4 fusion.33
  17.7 2.4 %collective-permute-start.2 = (bf16[256]{0:T(256)(128)(2,1)}, bf16[256]{0:T(256)(128)(2,1)}, u32[]{:S(2)}, u32[]{:S(2)}) collective-permute-start(bf16[256]{0:T(256)(128)(2,1)} %get-tuple-element.10), channel_id=1, source_target_pairs={{256,0},{264,8},{272,16},{280,24},{288,32},{296,40},{304,48},{312,... | collective-permute-start | bytes 1544 | tf_op jit(solution)/shard_map/ppermute | solution.py:19
  20.2 1.2 fusion.35
  21.4 3.4 %collective-permute-start = (bf16[256]{0:T(256)(128)(2,1)}, bf16[256]{0:T(256)(128)(2,1)}, u32[]{:S(2)}, u32[]{:S(2)}) collective-permute-start(bf16[256]{0:T(256)(128)(2,1)} %fusion.35), channel_id=1, source_target_pairs={{256,0},{264,8},{272,16},{280,24},{288,32},{296,40},{304,48},{312,... | collective-permute-start | bytes 1544 | tf_op jit(solution)/shard_map/ppermute | solution.py:19
  24.8 1.1 dynamic-slice_bitcast_fusion
  25.9 2.4 %collective-permute-start.3 = (bf16[1024,256]{1,0:T(8,128)(2,1)S(1)}, bf16[1024,256]{1,0:T(8,128)(2,1)}, u32[]{:S(2)}, u32[]{:S(2)}) collective-permute-start(bf16[1024,256]{1,0:T(8,128)(2,1)S(1)} %dynamic-slice_bitcast_fusion), channel_id=1, source_target_pairs={{256,0},{264,8},{272,16},{280,24},{288,32},{296,40},{304,48},{312,... | collective-permute-start | bytes 1572872 | tf_op jit(solution)/shard_map/ppermute | solution.py:19
  28.9 3.4 %collective-permute-start.4 = (bf16[256]{0:T(256)(128)(2,1)}, bf16[256]{0:T(256)(128)(2,1)}, u32[]{:S(2)}, u32[]{:S(2)}) collective-permute-start(bf16[256]{0:T(256)(128)(2,1)} %get-tuple-element.12), channel_id=1, source_target_pairs={{256,0},{264,8},{272,16},{280,24},{288,32},{296,40},{304,48},{312,... | collective-permute-start | bytes 1544 | tf_op jit(solution)/shard_map/ppermute | solution.py:19
  38.1 1.0 constant_dynamic-slice_fusion.6
  41.2 1.8 copy.50
  43.0 2.0 %fusion.24 = (f32[260]{0:T(512)S(1)}, f32[260]{0:T(512)S(1)}) fusion(s32[4]{0:T(128)S(1)} %iota.55, s32[256]{0:T(256)} %get-tuple-element.30, s32[]{:T(128)} %bitcast.6, s32[256]{0:T(256)} %get-tuple-element.29, s32[]{:T(128)} %bitcast.15), kind=kLoop, calls=%fused_computation.60 | loop fusion | flops 1560 | bytes 4152 | tf_op jit(solution)/shard_map/convert_element_type | solution.py:74
  45.0 1.5 pad_maximum_fusion.2
  46.5 3.0 %subtract_select_fusion = f32[2,512,512]{1,2,0:T(8,128)} fusion(f32[512,512]{0,1:T(8,128)S(1)} %subtract_convert_fusion, f32[2]{0:T(128)} %multiply_exponential_fusion, pred[512,512]{0,1:T(8,128)(4,1)S(1)} %fusion.2, bf16[512,256]{1,0:T(8,128)(2,1)} %param.17, bf16[512,256]{1,0:T(8,128)(2,1)} %param.16), kind=kOutput, calls=%fused_computation.3 | convolution fusion | flops 136314880 | bytes 3932168 | tf_op jit(solution)/shard_map/qhd,khd->hqk/dot_general | solution.py:40
  49.5 2.0 %fusion.48 = f32[2,512]{1,0:T(2,128)S(1)} fusion(f32[512,512]{0,1:T(8,128)S(1)} %subtract_convert_fusion, f32[2]{0:T(128)S(1)} %copy-done.4, pred[512,512]{0,1:T(8,128)(4,1)S(1)} %fusion.2, bf16[512,256]{1,0:T(8,128)(2,1)} %param.17, bf16[512,256]{1,0:T(8,128)(2,1)} %param.16), kind=kOutput, calls=%fused_computation.90 | convolution fusion | flops 137363968 | bytes 1839112 | tf_op jit(solution)/shard_map/sub | solution.py:30
  51.6 3.0 %convolution_convert_fusion = bf16[2,512,128]{1,2,0:T(8,128)(2,1)S(1)} fusion(bf16[512,2,128]{0,2,1:T(8,128)(2,1)} %bitcast.98, f32[2,512]{1,0:T(2,128)S(1)} %fusion.48, f32[2,512,512]{1,2,0:T(8,128)} %subtract_select_fusion), kind=kOutput, calls=%fused_computation.6 | convolution fusion | flops 135923200 | bytes 2625536 | tf_op jit(solution)/shard_map/hqk,khd->qhd/dot_general | solution.py:49
  54.6 0.9 constant_dynamic-slice_fusion.3
  58.9 0.9 constant_dynamic-slice_fusion.1
  65.0 75.5 %all-gather.2.cloned.1.call-done = bf16[514,2048]{0,1:T(8,128)(2,1)} async-done(((bf16[514,256]{0,1:T(8,128)(2,1)}), bf16[514,2048]{0,1:T(8,128)(2,1)}) %all-gather.2.cloned.1.call-update) | async-done | bytes 2105360 | tf_op jit(solution)/shard_map/all_gather | solution.py:135
  140.5 2.7 %fusion.53 = (f32[514]{0:T(1024)S(1)}, f32[514,256]{1,0:T(8,128)S(1)}) fusion(bf16[514,256]{1,0:T(8,128)(2,1)S(1)} %copy-done.8, f32[256]{0:T(256)S(1)} %copy-done.9, bf16[514,2048]{0,1:T(8,128)(2,1)} %all-gather.2.cloned.1.call-done, bf16[2048,256]{1,0:T(8,128)(2,1)S(1)} %copy-done), kind=kOutput, calls=%fused_computation.91 | convolution fusion | flops 539493888 | bytes 3946504 | tf_op jit(solution)/shard_map/dot_general | solution.py:134
  143.2 19.9 %psum.14 = f32[514]{0:T(1024)S(1)} all-reduce(f32[514]{0:T(1024)S(1)} %get-tuple-element.27), channel_id=1, replica_groups=mesh['rep'=64,'tp'=8] {'tp'}, use_global_device_ids=true, to_apply=%region_7.8 | all-reduce | flops 514 | bytes 4112 | tf_op jit(solution)/shard_map/psum | solution.py:142
  163.3 21.8 %psum.15 = f32[514]{0:T(1024)S(1)} all-reduce(f32[514]{0:T(1024)S(1)} %multiply_reduce_fusion), channel_id=1, replica_groups=mesh['rep'=64,'tp'=8] {'tp'}, use_global_device_ids=true, to_apply=%region_9.10 | all-reduce | flops 514 | bytes 4112 | tf_op jit(solution)/shard_map/psum | solution.py:144
  185.1 1.0 add_convert_fusion
  (75 shorter events, 13.4 us)
Async XLA Ops:
  7.2 133.3 %copy-start = (bf16[2048,256]{1,0:T(8,128)(2,1)S(1)}, bf16[2048,256]{1,0:T(8,128)(2,1)}, u32[]{:S(2)}) copy-start(bf16[2048,256]{1,0:T(8,128)(2,1)} %param.27) | copy-start | bytes 3145732
  7.2 21.1 %copy-start.3 = (bf16[2,256]{1,0:T(2,128)(2,1)S(1)}, bf16[2,256]{1,0:T(2,128)(2,1)}, u32[]{:S(2)}) copy-start(bf16[2,256]{1,0:T(2,128)(2,1)} %param.24) | copy-start | bytes 3076
  7.2 25.8 %copy-start.5 = (s32[128]{0:T(128)S(1)}, s32[128]{0:T(128)}, u32[]{:S(2)}) copy-start(s32[128]{0:T(128)} %param.25) | copy-start | bytes 1540
  7.2 133.3 %all-gather.2.cloned.1.call-start = ((), (), s32[]{:S(2)}) async-start(), calls=%async_computation | async-start | bytes 2949120 | tf_op jit(solution)/shard_map/all_gather | solution.py:135
  10.5 29.0 %copy-start.2 = (bf16[2,256]{1,0:T(2,128)(2,1)S(1)}, bf16[2,256]{1,0:T(2,128)(2,1)}, u32[]{:S(2)}) copy-start(bf16[2,256]{1,0:T(2,128)(2,1)} %param.22) | copy-start | bytes 3076
  11.6 42.9 %collective-permute-start.1 = (bf16[1024,256]{1,0:T(8,128)(2,1)S(1)}, bf16[1024,256]{1,0:T(8,128)(2,1)}, u32[]{:S(2)}, u32[]{:S(2)}) collective-permute-start(bf16[1024,256]{1,0:T(8,128)(2,1)S(1)} %dynamic-slice_bitcast_fusion.1), channel_id=1, source_target_pairs={{256,0},{264,8},{272,16},{280,24},{288,32},{296,40},{304,48},{312,... | collective-permute-start | bytes 1572872 | tf_op jit(solution)/shard_map/ppermute | solution.py:19
  17.7 38.7 %collective-permute-start.2 = (bf16[256]{0:T(256)(128)(2,1)}, bf16[256]{0:T(256)(128)(2,1)}, u32[]{:S(2)}, u32[]{:S(2)}) collective-permute-start(bf16[256]{0:T(256)(128)(2,1)} %get-tuple-element.10), channel_id=1, source_target_pairs={{256,0},{264,8},{272,16},{280,24},{288,32},{296,40},{304,48},{312,... | collective-permute-start | bytes 1544 | tf_op jit(solution)/shard_map/ppermute | solution.py:19
  21.4 35.8 %collective-permute-start = (bf16[256]{0:T(256)(128)(2,1)}, bf16[256]{0:T(256)(128)(2,1)}, u32[]{:S(2)}, u32[]{:S(2)}) collective-permute-start(bf16[256]{0:T(256)(128)(2,1)} %fusion.35), channel_id=1, source_target_pairs={{256,0},{264,8},{272,16},{280,24},{288,32},{296,40},{304,48},{312,... | collective-permute-start | bytes 1544 | tf_op jit(solution)/shard_map/ppermute | solution.py:19
  25.9 33.0 %collective-permute-start.3 = (bf16[1024,256]{1,0:T(8,128)(2,1)S(1)}, bf16[1024,256]{1,0:T(8,128)(2,1)}, u32[]{:S(2)}, u32[]{:S(2)}) collective-permute-start(bf16[1024,256]{1,0:T(8,128)(2,1)S(1)} %dynamic-slice_bitcast_fusion), channel_id=1, source_target_pairs={{256,0},{264,8},{272,16},{280,24},{288,32},{296,40},{304,48},{312,... | collective-permute-start | bytes 1572872 | tf_op jit(solution)/shard_map/ppermute | solution.py:19
  28.9 31.9 %collective-permute-start.4 = (bf16[256]{0:T(256)(128)(2,1)}, bf16[256]{0:T(256)(128)(2,1)}, u32[]{:S(2)}, u32[]{:S(2)}) collective-permute-start(bf16[256]{0:T(256)(128)(2,1)} %get-tuple-element.12), channel_id=1, source_target_pairs={{256,0},{264,8},{272,16},{280,24},{288,32},{296,40},{304,48},{312,... | collective-permute-start | bytes 1544 | tf_op jit(solution)/shard_map/ppermute | solution.py:19
  46.5 3.0 %copy-start.4 = (f32[2]{0:T(128)S(1)}, f32[2]{0:T(128)}, u32[]{:S(2)}) copy-start(f32[2]{0:T(128)} %multiply_exponential_fusion) | copy-start | bytes 28
  51.6 6.9 %copy-start.1 = (bf16[260,2,128]{2,1,0:T(2,128)(2,1)S(1)}, bf16[260,2,128]{2,1,0:T(2,128)(2,1)}, u32[]{:S(2)}) copy-start(bf16[260,2,128]{2,1,0:T(2,128)(2,1)} %pad_maximum_fusion.2) | copy-start | bytes 399364
  57.2 83.3 %copy-start.8 = (bf16[514,256]{1,0:T(8,128)(2,1)S(1)}, bf16[514,256]{1,0:T(8,128)(2,1)}, u32[]{:S(2)}) copy-start(bf16[514,256]{1,0:T(8,128)(2,1)} %param.29) | copy-start | bytes 789508
  57.2 83.3 %copy-start.9 = (f32[256]{0:T(256)S(1)}, f32[256]{0:T(256)}, u32[]{:S(2)}) copy-start(f32[256]{0:T(256)} %param.28) | copy-start | bytes 3076
  65.0 120.1 %copy-start.6 = (f32[256]{0:T(256)S(1)}, f32[256]{0:T(256)}, u32[]{:S(2)}) copy-start(f32[256]{0:T(256)} %param.31) | copy-start | bytes 3076
  65.0 120.1 %copy-start.7 = (f32[256]{0:T(256)S(1)}, f32[256]{0:T(256)}, u32[]{:S(2)}) copy-start(f32[256]{0:T(256)} %param.30) | copy-start | bytes 3076
Sparse Core Ops, SparseCore 0:
  62.9 77.5 all-gather.1
where the time goes:
time: 194 us; the launch traced here: 193 us
  waiting for transfers between devices  75.5 us (39%)
  blocking collectives  41.6 us (21%)
  between operations  21.3 us (11%)
  local copies, waits for them, and re-layouts  17.8 us (9%)
  starting transfers between devices  15.1 us (8%)
  matrix products  11.9 us (6%)
  other arithmetic  9.62 us (5%)
    all_gather x1, waiting for transfers between devices, on_device(): lax.all_gather(mixed_rows, 'tp', axis=1, tiled=True)  75.5 us
    psum x1, blocking collectives, on_device(): row_var = lax.psum(jnp.sum(centered * centered, axis=1), 'tp') / D  21.8 us
    psum x1, blocking collectives, on_device(): row_mean = lax.psum(row_total, 'tp') / D  19.9 us
    ppermute x5, starting transfers between devices, from_behind(): return lax.ppermute(block, axis, route)  15.1 us
  transfers between devices with their start and end apart: 6, of which 1 were waited for; matrix products, arithmetic and copies ran while one was open for 16% of the time, Pallas kernels for 0%

commit v1 on v0

--- a/solution.py
+++ b/solution.py
@@ -1,8 +1,10 @@
+import functools
 import math
 import jax
 import jax.numpy as jnp
 from jax import lax
 from jax.sharding import PartitionSpec as P
+from jax.lax import all_gather
 
 D = 2048
 HEADS = 16
@@ -11,6 +13,13 @@
 WIN = 256
 masked_score = -1e30
 norm_epsilon = 1e-05
+
+
+def finish_lots_all(vector, comm_axis):
+    return all_gather(vector, comm_axis).sum(axis=0)
+
+
+_render_links = functools.partial(finish_lots_all, comm_axis="tp")
 
 
 def from_behind(block, axis, distance):
@@ -141,7 +150,7 @@
     row_total = jnp.sum(stream, axis=1)
     row_mean = lax.psum(row_total, "tp") / D
     centered = stream - row_mean[:, None]
-    row_var = lax.psum(jnp.sum(centered * centered, axis=1), "tp") / D
+    row_var = _render_links(jnp.sum(centered * centered, axis=1)) / D
     normed = (
         centered * lax.rsqrt(row_var + norm_epsilon)[:, None] * ln_gain[None, :] + ln_shift[None, :]
     ).astype(jnp.bfloat16)

time: 194 us -> 212 us (1.093)
  blocking collectives: 41.6 us -> 59.2 us
    unnamed x0 -> x1, blocking collectives: none -> 39.4 us
    psum x1 -> x0, blocking collectives: 21.8 us -> none  [on_device(): row_var = lax.psum(jnp.sum(centered * centered, axis=1), 'tp') / D]
  transfers between devices with their start and end apart: 6 -> 6, of which waited for: 1 -> 1; matrix products, arithmetic and copies ran while one was open for 16% -> 15% of each run, Pallas kernels for 0% -> 0%
where the time goes in v1:
time: 212 us; the launch traced here: 211 us
  waiting for transfers between devices  73.6 us (35%)
  blocking collectives  59.2 us (28%)
  between operations  22 us (10%)
  local copies, waits for them, and re-layouts  19.5 us (9%)
  starting transfers between devices  15.1 us (7%)
  matrix products  11.9 us (6%)
  other arithmetic  9.63 us (5%)
    all_gather x1, waiting for transfers between devices, on_device(): lax.all_gather(mixed_rows, 'tp', axis=1, tiled=True)  73.6 us
    unnamed x1, blocking collectives  39.4 us
    psum x1, blocking collectives, on_device(): row_mean = lax.psum(row_total, 'tp') / D  19.9 us
    ppermute x5, starting transfers between devices, from_behind(): return lax.ppermute(block, axis, route)  15.1 us
  transfers between devices with their start and end apart: 6, of which 1 were waited for; matrix products, arithmetic and copies ran while one was open for 15% of the time, Pallas kernels for 0%

profile of v1, /device:TPU:32, one launch (start us, length us, event | category | flops | bytes accessed | tf_op | source)
XLA Modules:
  0.0 211.0 jit_solution(7276000116194837077)
XLA Ops:
  7.3 1.3 fusion.47
  10.6 1.1 dynamic-slice_bitcast_fusion.1
  11.6 3.4 %collective-permute-start.1 = (bf16[1024,256]{1,0:T(8,128)(2,1)S(1)}, bf16[1024,256]{1,0:T(8,128)(2,1)}, u32[]{:S(2)}, u32[]{:S(2)}) collective-permute-start(bf16[1024,256]{1,0:T(8,128)(2,1)S(1)} %dynamic-slice_bitcast_fusion.1), channel_id=1, source_target_pairs={{256,0},{264,8},{272,16},{280,24},{288,32},{296,40},{304,48},{312,... | collective-permute-start | bytes 1572872 | tf_op jit(solution)/shard_map/ppermute | solution.py:28
  16.3 1.4 fusion.33
  17.7 2.4 %collective-permute-start.2 = (bf16[256]{0:T(256)(128)(2,1)}, bf16[256]{0:T(256)(128)(2,1)}, u32[]{:S(2)}, u32[]{:S(2)}) collective-permute-start(bf16[256]{0:T(256)(128)(2,1)} %get-tuple-element.10), channel_id=1, source_target_pairs={{256,0},{264,8},{272,16},{280,24},{288,32},{296,40},{304,48},{312,... | collective-permute-start | bytes 1544 | tf_op jit(solution)/shard_map/ppermute | solution.py:28
  20.2 1.2 fusion.35
  21.4 3.4 %collective-permute-start = (bf16[256]{0:T(256)(128)(2,1)}, bf16[256]{0:T(256)(128)(2,1)}, u32[]{:S(2)}, u32[]{:S(2)}) collective-permute-start(bf16[256]{0:T(256)(128)(2,1)} %fusion.35), channel_id=1, source_target_pairs={{256,0},{264,8},{272,16},{280,24},{288,32},{296,40},{304,48},{312,... | collective-permute-start | bytes 1544 | tf_op jit(solution)/shard_map/ppermute | solution.py:28
  24.8 1.1 dynamic-slice_bitcast_fusion
  25.9 2.4 %collective-permute-start.3 = (bf16[1024,256]{1,0:T(8,128)(2,1)S(1)}, bf16[1024,256]{1,0:T(8,128)(2,1)}, u32[]{:S(2)}, u32[]{:S(2)}) collective-permute-start(bf16[1024,256]{1,0:T(8,128)(2,1)S(1)} %dynamic-slice_bitcast_fusion), channel_id=1, source_target_pairs={{256,0},{264,8},{272,16},{280,24},{288,32},{296,40},{304,48},{312,... | collective-permute-start | bytes 1572872 | tf_op jit(solution)/shard_map/ppermute | solution.py:28
  28.9 3.4 %collective-permute-start.4 = (bf16[256]{0:T(256)(128)(2,1)}, bf16[256]{0:T(256)(128)(2,1)}, u32[]{:S(2)}, u32[]{:S(2)}) collective-permute-start(bf16[256]{0:T(256)(128)(2,1)} %get-tuple-element.12), channel_id=1, source_target_pairs={{256,0},{264,8},{272,16},{280,24},{288,32},{296,40},{304,48},{312,... | collective-permute-start | bytes 1544 | tf_op jit(solution)/shard_map/ppermute | solution.py:28
  38.1 1.0 constant_dynamic-slice_fusion.6
  41.2 1.8 copy.50
  43.0 2.0 fusion.24
  45.0 1.5 pad_maximum_fusion.2
  46.5 3.0 %subtract_select_fusion = f32[2,512,512]{1,2,0:T(8,128)} fusion(f32[512,512]{0,1:T(8,128)S(1)} %subtract_convert_fusion, f32[2]{0:T(128)} %multiply_exponential_fusion, pred[512,512]{0,1:T(8,128)(4,1)S(1)} %fusion.2, bf16[512,256]{1,0:T(8,128)(2,1)} %param.17, bf16[512,256]{1,0:T(8,128)(2,1)} %param.16), kind=kOutput, calls=%fused_computation.3 | convolution fusion | flops 136314880 | bytes 3932168 | tf_op jit(solution)/shard_map/qhd,khd->hqk/dot_general | solution.py:49
  49.5 2.0 fusion.48
  51.6 3.0 %convolution_convert_fusion = bf16[2,512,128]{1,2,0:T(8,128)(2,1)S(1)} fusion(bf16[512,2,128]{0,2,1:T(8,128)(2,1)} %bitcast.99, f32[2,512]{1,0:T(2,128)S(1)} %fusion.48, f32[2,512,512]{1,2,0:T(8,128)} %subtract_select_fusion), kind=kOutput, calls=%fused_computation.6 | convolution fusion | flops 135923200 | bytes 2625536 | tf_op jit(solution)/shard_map/hqk,khd->qhd/dot_general | solution.py:58
  54.6 0.9 constant_dynamic-slice_fusion.3
  62.8 1.3 dynamic-slice.4
  66.9 73.6 %all-gather.3.cloned.1.call-done = bf16[514,2048]{0,1:T(8,128)(2,1)} async-done(((bf16[514,256]{0,1:T(8,128)(2,1)}), bf16[514,2048]{0,1:T(8,128)(2,1)}) %all-gather.3.cloned.1.call-update) | async-done | bytes 2105360 | tf_op jit(solution)/shard_map/all_gather | solution.py:144
  140.5 2.7 %fusion.53 = (f32[514]{0:T(1024)S(1)}, f32[514,256]{1,0:T(8,128)S(1)}) fusion(bf16[514,256]{1,0:T(8,128)(2,1)S(1)} %copy-done.8, f32[256]{0:T(256)S(1)} %copy-done.9, bf16[514,2048]{0,1:T(8,128)(2,1)} %all-gather.3.cloned.1.call-done, bf16[2048,256]{1,0:T(8,128)(2,1)S(1)} %copy-done), kind=kOutput, calls=%fused_computation.91 | convolution fusion | flops 539493888 | bytes 3946504 | tf_op jit(solution)/shard_map/dot_general | solution.py:143
  143.2 19.9 %psum.7 = f32[514]{0:T(1024)S(1)} all-reduce(f32[514]{0:T(1024)S(1)} %get-tuple-element.27), channel_id=1, replica_groups=mesh['rep'=64,'tp'=8] {'tp'}, use_global_device_ids=true, to_apply=%region_7.8 | all-reduce | flops 514 | bytes 4112 | tf_op jit(solution)/shard_map/psum | solution.py:151
  163.7 39.4 %all-reduce = f32[4112]{0:T(1024)S(1)} all-reduce(f32[4112]{0:T(1024)S(1)} %dynamic-update-slice), channel_id=2, replica_groups=mesh['rep'=64,'tp'=8] {'tp'}, use_global_device_ids=true, to_apply=%add | all-reduce | flops 4112 | bytes 32896
  203.2 1.0 add_convert_fusion
  (80 shorter events, 14.7 us)
Async XLA Ops:
  7.2 133.3 %copy-start = (bf16[2048,256]{1,0:T(8,128)(2,1)S(1)}, bf16[2048,256]{1,0:T(8,128)(2,1)}, u32[]{:S(2)}) copy-start(bf16[2048,256]{1,0:T(8,128)(2,1)} %param.27) | copy-start | bytes 3145732
  7.2 21.1 %copy-start.3 = (bf16[2,256]{1,0:T(2,128)(2,1)S(1)}, bf16[2,256]{1,0:T(2,128)(2,1)}, u32[]{:S(2)}) copy-start(bf16[2,256]{1,0:T(2,128)(2,1)} %param.24) | copy-start | bytes 3076
  7.2 25.8 %copy-start.5 = (s32[128]{0:T(128)S(1)}, s32[128]{0:T(128)}, u32[]{:S(2)}) copy-start(s32[128]{0:T(128)} %param.25) | copy-start | bytes 1540
  7.2 133.3 %all-gather.3.cloned.1.call-start = ((), (), s32[]{:S(2)}) async-start(), calls=%async_computation | async-start | bytes 2949120 | tf_op jit(solution)/shard_map/all_gather | solution.py:144
  10.5 29.0 %copy-start.2 = (bf16[2,256]{1,0:T(2,128)(2,1)S(1)}, bf16[2,256]{1,0:T(2,128)(2,1)}, u32[]{:S(2)}) copy-start(bf16[2,256]{1,0:T(2,128)(2,1)} %param.22) | copy-start | bytes 3076
  11.6 42.9 %collective-permute-start.1 = (bf16[1024,256]{1,0:T(8,128)(2,1)S(1)}, bf16[1024,256]{1,0:T(8,128)(2,1)}, u32[]{:S(2)}, u32[]{:S(2)}) collective-permute-start(bf16[1024,256]{1,0:T(8,128)(2,1)S(1)} %dynamic-slice_bitcast_fusion.1), channel_id=1, source_target_pairs={{256,0},{264,8},{272,16},{280,24},{288,32},{296,40},{304,48},{312,... | collective-permute-start | bytes 1572872 | tf_op jit(solution)/shard_map/ppermute | solution.py:28
  17.7 38.7 %collective-permute-start.2 = (bf16[256]{0:T(256)(128)(2,1)}, bf16[256]{0:T(256)(128)(2,1)}, u32[]{:S(2)}, u32[]{:S(2)}) collective-permute-start(bf16[256]{0:T(256)(128)(2,1)} %get-tuple-element.10), channel_id=1, source_target_pairs={{256,0},{264,8},{272,16},{280,24},{288,32},{296,40},{304,48},{312,... | collective-permute-start | bytes 1544 | tf_op jit(solution)/shard_map/ppermute | solution.py:28
  21.4 35.8 %collective-permute-start = (bf16[256]{0:T(256)(128)(2,1)}, bf16[256]{0:T(256)(128)(2,1)}, u32[]{:S(2)}, u32[]{:S(2)}) collective-permute-start(bf16[256]{0:T(256)(128)(2,1)} %fusion.35), channel_id=1, source_target_pairs={{256,0},{264,8},{272,16},{280,24},{288,32},{296,40},{304,48},{312,... | collective-permute-start | bytes 1544 | tf_op jit(solution)/shard_map/ppermute | solution.py:28
  25.9 33.0 %collective-permute-start.3 = (bf16[1024,256]{1,0:T(8,128)(2,1)S(1)}, bf16[1024,256]{1,0:T(8,128)(2,1)}, u32[]{:S(2)}, u32[]{:S(2)}) collective-permute-start(bf16[1024,256]{1,0:T(8,128)(2,1)S(1)} %dynamic-slice_bitcast_fusion), channel_id=1, source_target_pairs={{256,0},{264,8},{272,16},{280,24},{288,32},{296,40},{304,48},{312,... | collective-permute-start | bytes 1572872 | tf_op jit(solution)/shard_map/ppermute | solution.py:28
  28.9 31.9 %collective-permute-start.4 = (bf16[256]{0:T(256)(128)(2,1)}, bf16[256]{0:T(256)(128)(2,1)}, u32[]{:S(2)}, u32[]{:S(2)}) collective-permute-start(bf16[256]{0:T(256)(128)(2,1)} %get-tuple-element.12), channel_id=1, source_target_pairs={{256,0},{264,8},{272,16},{280,24},{288,32},{296,40},{304,48},{312,... | collective-permute-start | bytes 1544 | tf_op jit(solution)/shard_map/ppermute | solution.py:28
  46.5 3.0 %copy-start.4 = (f32[2]{0:T(128)S(1)}, f32[2]{0:T(128)}, u32[]{:S(2)}) copy-start(f32[2]{0:T(128)} %multiply_exponential_fusion) | copy-start | bytes 28
  51.6 6.9 %copy-start.1 = (bf16[260,2,128]{2,1,0:T(2,128)(2,1)S(1)}, bf16[260,2,128]{2,1,0:T(2,128)(2,1)}, u32[]{:S(2)}) copy-start(bf16[260,2,128]{2,1,0:T(2,128)(2,1)} %pad_maximum_fusion.2) | copy-start | bytes 399364
  57.2 83.3 %copy-start.8 = (bf16[514,256]{1,0:T(8,128)(2,1)S(1)}, bf16[514,256]{1,0:T(8,128)(2,1)}, u32[]{:S(2)}) copy-start(bf16[514,256]{1,0:T(8,128)(2,1)} %param.29) | copy-start | bytes 789508
  57.2 83.3 %copy-start.9 = (f32[256]{0:T(256)S(1)}, f32[256]{0:T(256)}, u32[]{:S(2)}) copy-start(f32[256]{0:T(256)} %param.28) | copy-start | bytes 3076
  66.9 136.2 %copy-start.6 = (f32[256]{0:T(256)S(1)}, f32[256]{0:T(256)}, u32[]{:S(2)}) copy-start(f32[256]{0:T(256)} %param.31) | copy-start | bytes 3076
  66.9 136.3 %copy-start.7 = (f32[256]{0:T(256)S(1)}, f32[256]{0:T(256)}, u32[]{:S(2)}) copy-start(f32[256]{0:T(256)} %param.30) | copy-start | bytes 3076
Sparse Core Ops, SparseCore 0:
  62.9 77.5 all-gather.2
